TPU v7x, 32 devices: a whole 2x2x4 slice. The times are simulated.
32 devices in a mesh: dp: 4 (over z), tp: 8 (over y, x, core).
Axes of the slice: x: 2, y: 2, z: 4, core: 2. Of those that a mesh axis runs over, the one named last changes fastest.
Arguments:
- head_fsdp: bfloat16 [4096, 128256], P(('dp', 'tp')), may hold values from -0.5 to 0.5
- hidden: bfloat16 [1024, 4096], P(('dp', 'tp')), may hold values from -48 to 48
- targets: int32 [1024], P(('dp', 'tp')), may hold values from 0 to 128255
Outputs:
- head_tp: bfloat16 [4096, 128256], P('dp', 'tp')
- log_norm: float32 [1024], P(('dp', 'tp'))
- target_logprob: float32 [1024], P(('dp', 'tp'))
All inputs are finite; a program needn't handle non-finite values.
Results may differ from a plain program's by a relative error of at most 0.0004.
Values may be sent and summed in bfloat16 or wider, within the bound.
A program may use at most 256 MiB of HBM per device.

v0:
```python
import jax
import jax.numpy as jnp
from jax import lax
from jax.sharding import PartitionSpec as P


def shards(head_fsdp, hidden, targets):
    head_tp = lax.all_to_all(head_fsdp, "tp", split_axis=1, concat_axis=0, tiled=True)
    head_full = lax.all_to_all(head_fsdp, ("dp", "tp"), split_axis=1, concat_axis=0, tiled=True)
    vocab_start = (
        lax.axis_index("dp") * lax.axis_size("tp") + lax.axis_index("tp")
    ) * head_full.shape[1]
    all_hidden, all_targets = (
        lax.all_gather(hidden, ("dp", "tp"), axis=0, tiled=True),
        lax.all_gather(targets, ("dp", "tp"), axis=0, tiled=True),
    )
    logits = jnp.dot(all_hidden, head_full, preferred_element_type=jnp.float32)
    local_peak = jnp.max(logits, axis=1)
    offset = all_targets - vocab_start
    columns = lax.broadcasted_iota(jnp.int32, logits.shape, 1)
    picked = jnp.sum(jnp.where(columns == offset[:, None], logits, 0.0), axis=1)
    top_logit = lax.pmax(local_peak, ("dp", "tp"))
    local_mass = jnp.sum(jnp.exp(logits - top_logit[:, None]), axis=1)
    total_mass, target_logit = lax.psum((local_mass, picked), ("dp", "tp"))
    log_norm = top_logit + jnp.log(total_mass)
    logprob = target_logit - log_norm
    own_rows = hidden.shape[0]
    row_start = (lax.axis_index("dp") * lax.axis_size("tp") + lax.axis_index("tp")) * own_rows
    own_norm = lax.dynamic_slice_in_dim(log_norm, row_start, own_rows, 0)
    own_logprob = lax.dynamic_slice_in_dim(logprob, row_start, own_rows, 0)
    return (head_tp, own_norm, own_logprob)


def solution(mesh):
    in_specs = (P(("dp", "tp"), None), P(("dp", "tp"), None), P(("dp", "tp")))
    out_specs = (P("dp", "tp"), P(("dp", "tp")), P(("dp", "tp")))
    return jax.shard_map(shards, mesh=mesh, in_specs=in_specs, out_specs=out_specs, check_vma=False)
```

profile of v0, /device:TPU:0, one launch (start us, length us, event | category | flops | bytes accessed | tf_op | source)
XLA Modules:
  0.0 1462.2 jit_solution(3850153198635637971)
XLA Ops:
  7.2 42.5 %copy.10 = bf16[128,128256]{0,1:T(8,128)(2,1)} copy(bf16[128,128256]{1,0:T(8,128)(2,1)} %param.3) | data formatting | bytes 65667072 | tf_op args[0]
  49.7 367.6 %all_to_all.38 = bf16[128,8,16032]{0,2,1:T(8,128)(2,1)} all-to-all(bf16[128,8,16032]{0,2,1:T(8,128)(2,1)} %bitcast.8), channel_id=1, replica_groups=mesh['dp'=4,'tp'=8] {'tp'}, dimensions={1} | all-to-all | bytes 65667072 | tf_op jit(solution)/shard_map/all_to_all | solution.py:8
  417.3 0.0 copy-start
  417.3 4.8 all-to-all-start.1
  422.1 0.0 all-gather.2.cloned.1.call-start
  422.2 0.7 all-gather.2.cloned.1.call-update
  422.9 0.0 copy-done
  422.9 0.2 dynamic-update-slice
  423.1 778.6 %all-reduce = s32[1024]{0:T(1024)S(1)} all-reduce(s32[1024]{0:T(1024)S(1)} %dynamic-update-slice), channel_id=1, replica_groups=mesh['dp'=4,'tp'=8] {'dp','tp'}, use_global_device_ids=true, to_apply=%add | all-reduce | flops 1024 | bytes 8192
  1201.8 38.6 %copy.11 = bf16[8,128,16032]{2,1,0:T(8,128)(2,1)} copy(bf16[8,128,16032]{1,2,0:T(8,128)(2,1)} %bitcast.11) | data formatting | bytes 65667072 | tf_op jit(solution)/shard_map/all_to_all | solution.py:8
  1240.4 42.5 %copy.14 = bf16[1024,16032]{0,1:T(8,128)(2,1)} copy(bf16[1024,16032]{1,0:T(8,128)(2,1)} %bitcast.10) | data formatting | bytes 65667072
  1282.9 0.0 all-to-all-done.1
  1282.9 41.0 %copy.13 = bf16[32,128,4008]{2,1,0:T(8,128)(2,1)} copy(bf16[32,128,4008]{1,2,0:T(8,128)(2,1)} %bitcast.4) | data formatting | bytes 65667072 | tf_op jit(solution)/shard_map/all_to_all | solution.py:9
  1323.9 0.0 all-gather.2.cloned.1.call-done
  1323.9 42.3 %fusion.1 = (f32[1024]{0:T(1024)S(1)}, f32[1024,4008]{0,1:T(8,128)}) fusion(bf16[1024,4096]{1,0:T(8,128)(2,1)} %all-gather.2.cloned.1.call-done, bf16[4096,4008]{1,0:T(8,128)(2,1)} %bitcast.12), kind=kOutput, calls=%fused_computation.6 | convolution fusion | flops 33625645056 | bytes 57643008 | tf_op jit(solution)/shard_map/dot_general | solution.py:17
  1366.2 37.9 %pmax.7 = f32[1024]{0:T(1024)S(1)} all-reduce(f32[1024]{0:T(1024)S(1)} %get-tuple-element.12), channel_id=1, replica_groups=mesh['dp'=4,'tp'=8] {'dp','tp'}, use_global_device_ids=true, to_apply=%region_1.2 | all-reduce | flops 1024 | bytes 8192 | tf_op jit(solution)/shard_map/pmax | solution.py:22
  1404.1 8.0 select_reduce_fusion
  1412.1 42.1 %all-reduce.1 = (f32[1024]{0:T(1024)S(1)}, f32[1024]{0:T(1024)S(1)}) all-reduce(f32[1024]{0:T(1024)S(1)} %get-tuple-element.7, f32[1024]{0:T(1024)S(1)} %get-tuple-element.6), channel_id=1, replica_groups=mesh['dp'=4,'tp'=8] {'dp','tp'}, use_global_device_ids=true, to_apply=%region_3.4 | all-reduce | flops 2048 | bytes 16384 | tf_op jit(solution)/shard_map/psum | solution.py:24
  1454.2 0.6 dynamic_slice.7
  1454.8 0.6 dynamic_slice.6
  (3 shorter events, 0.0 us)
Async XLA Ops:
  417.3 5.6 copy-start
  417.3 865.6 %all-to-all-start.1 = ((bf16[128,32,4008]{0,2,1:T(8,128)(2,1)}), bf16[128,32,4008]{0,2,1:T(8,128)(2,1)}, u32[]{:S(2)}, u32[]{:S(2)}) async-start(bf16[128,32,4008]{0,2,1:T(8,128)(2,1)} %bitcast.9), calls=%async_computation.1 | async-start | bytes 65667072 | tf_op jit(solution)/shard_map/all_to_all | solution.py:9
  422.1 901.7 %all-gather.2.cloned.1.call-start = ((), (), s32[]{:S(2)}) async-start(), calls=%async_computation.2 | async-start | bytes 8650752 | tf_op jit(solution)/shard_map/all_gather | solution.py:14
Sparse Core Ops, SparseCore 0:
  425.8 296.2 all-gather.1
where the time goes:
time: 1470 us; the launch traced here: 1460 us
  blocking collectives  1230 us (84%)
  local copies, waits for them, and re-layouts  166 us (11%)
  matrix products  42.3 us (3%)
    unnamed x1, blocking collectives  779 us
    all_to_all x1, blocking collectives, shards(): lax.all_to_all(head_fsdp, 'tp', split_axis=1, concat_axis=0, tiled=True)  368 us
    unnamed x6, local copies, waits for them, and re-layouts  85.3 us
    dot_general x1, matrix products, shards(): logits = jnp.dot(all_hidden, head_full, preferred_element_type=jnp.float32)  42.3 us
    psum x1, blocking collectives, shards(): total_mass, target_logit = lax.psum((local_mass, picked), ('dp', 'tp'))  42.1 us
    all_to_all x1, local copies, waits for them, and re-layouts, shards(): lax.all_to_all(head_fsdp, ('dp', 'tp'), split_axis=1, concat_axis=0, tile...  41 us
    all_to_all x1, local copies, waits for them, and re-layouts, shards(): lax.all_to_all(head_fsdp, 'tp', split_axis=1, concat_axis=0, tiled=True)  38.6 us
    pmax x1, blocking collectives, shards(): top_logit = lax.pmax(local_peak, ('dp', 'tp'))  37.9 us
  transfers between devices with their start and end apart: 2, of which 0 were waited for; matrix products, arithmetic and copies ran while one was open for 8% of the time, Pallas kernels for 0%

commit v1 on v0

--- a/solution.py
+++ b/solution.py
@@ -1,10 +1,266 @@
+import functools
+
 import jax
 import jax.numpy as jnp
 from jax import lax
+from jax.experimental import pallas as pl
+from jax.experimental.pallas import tpu as pltpu
 from jax.sharding import PartitionSpec as P
 
-
-def shards(head_fsdp, hidden, targets):
+MESH = pl.DeviceIdType.MESH
+CHUNKS = 8
+AHEAD = 3
+TILE = 512
+LOWEST = -3.0e38
+
+
+def round_up(n, m):
+    return -(-n // m) * m
+
+
+def plan(columns, n_dp, chunks):
+    share = round_up(-(-columns // (n_dp * chunks)), 8)
+    steps, start, place = [], 0, 0
+    while start < columns:
+        rows = min(share * n_dp, columns - start)
+        part = round_up(-(-rows // n_dp), 8)
+        steps.append((start, rows, part, place))
+        start += rows
+        place += part
+    return steps, place
+
+
+def part_start(peer, rows, part):
+    return pl.multiple_of(jnp.minimum(peer * part, rows - part), 8)
+
+
+def exchange(n_dp, n_tp, steps, head, hid, tgt, mid, full, all_hid, all_tgt, own_a, own_b, own_h, own_t,
+             a_send, a_recv, b_send, b_recv, h_send, h_recv, g_send, g_recv, local):
+    z, t = lax.axis_index("dp"), lax.axis_index("tp")
+    depth = hid.shape[0]
+    width = head.shape[1]
+    columns = mid.shape[0]
+    zs = [lax.rem(z + j, n_dp) for j in range(n_dp)]
+    ts = [lax.rem(t + j, n_tp) for j in range(n_tp)]
+    barrier = pltpu.get_barrier_semaphore()
+    for peer in zs[1:]:
+        pl.semaphore_signal(barrier, inc=1, device_id=(peer, t), device_id_type=MESH)
+    for peer in ts[1:]:
+        pl.semaphore_signal(barrier, inc=1, device_id=(z, peer), device_id_type=MESH)
+    n = len(steps)
+    lane = pl.ds(pl.multiple_of(t * width, width), width)
+    block = pl.ds(pl.multiple_of(z * mid.shape[1], mid.shape[1]), mid.shape[1])
+
+    loads = []
+    for c, (start, rows, part, place) in enumerate(steps):
+        copy = pltpu.make_async_copy(
+            head.at[pl.ds(pl.multiple_of(t * columns + start, 8), rows)], own_a.at[pl.ds(start, rows)], local.at[0, c])
+        copy.start()
+        loads.append(copy)
+    in_h = pltpu.make_async_copy(hid, own_h, local.at[4, 0])
+    in_t = pltpu.make_async_copy(tgt, own_t, local.at[4, 1])
+    in_h.start()
+    in_t.start()
+    pl.semaphore_wait(barrier, n_dp + n_tp - 2)
+
+    def send_a(c):
+        start, rows, part, place = steps[c]
+        copies = []
+        for j in range(1, n_tp):
+            copy = pltpu.make_async_remote_copy(
+                src_ref=head.at[pl.ds(pl.multiple_of(ts[j] * columns + start, 8), rows)],
+                dst_ref=mid.at[pl.ds(start, rows), lane],
+                send_sem=a_send.at[c, j - 1], recv_sem=a_recv.at[c, j - 1],
+                device_id=(z, ts[j]), device_id_type=MESH)
+            copy.start()
+            copies.append(copy)
+        return copies
+
+    sent_a = [send_a(c) for c in range(min(AHEAD, n))]
+
+    small = []
+    for j in range(1, n_dp):
+        for k, (src, dst) in enumerate(((hid, all_hid), (tgt, all_tgt))):
+            copy = pltpu.make_async_remote_copy(
+                src_ref=src, dst_ref=dst.at[t, z], send_sem=h_send.at[k, j - 1], recv_sem=h_recv.at[k, j - 1],
+                device_id=(zs[j], t), device_id_type=MESH)
+            copy.start()
+            small.append(copy)
+    in_h.wait()
+    in_t.wait()
+    out_h = pltpu.make_async_copy(own_h, all_hid.at[t, z], local.at[4, 2])
+    out_t = pltpu.make_async_copy(own_t, all_tgt.at[t, z], local.at[4, 3])
+    out_h.start()
+    out_t.start()
+    stores = []
+    for c, (start, rows, part, place) in enumerate(steps):
+        loads[c].wait()
+        copy = pltpu.make_async_copy(own_a.at[pl.ds(start, rows)], mid.at[pl.ds(start, rows), lane], local.at[1, c])
+        copy.start()
+        stores.append(copy)
+
+    sent_b, ins_b, outs_b, spread = [], [], [], []
+
+    def keep_b(c):
+        start, rows, part, place = steps[c]
+        ins_b[c].wait()
+        copy = pltpu.make_async_copy(own_b.at[pl.ds(place, part)], full.at[pl.ds(place, part), block], local.at[3, c])
+        copy.start()
+        outs_b.append(copy)
+
+    for c, (start, rows, part, place) in enumerate(steps):
+        stores[c].wait()
+        for copy in sent_a[c]:
+            copy.wait_recv()
+        for j in range(1, n_dp):
+            copy = pltpu.make_async_remote_copy(
+                src_ref=mid.at[pl.ds(start + part_start(zs[j], rows, part), part)],
+                dst_ref=full.at[pl.ds(place, part), block],
+                send_sem=b_send.at[c, j - 1], recv_sem=b_recv.at[c, j - 1],
+                device_id=(zs[j], t), device_id_type=MESH)
+            copy.start()
+            sent_b.append(copy)
+        copy = pltpu.make_async_copy(
+            mid.at[pl.ds(start + part_start(z, rows, part), part)], own_b.at[pl.ds(place, part)], local.at[2, c])
+        copy.start()
+        ins_b.append(copy)
+        if c + AHEAD < n:
+            sent_a.append(send_a(c + AHEAD))
+        if c >= 1:
+            keep_b(c - 1)
+        if c == min(1, n - 1):
+            out_h.wait()
+            out_t.wait()
+            for copy in small:
+                copy.wait_recv()
+            for j in range(1, n_tp):
+                for k, ref in enumerate((all_hid, all_tgt)):
+                    copy = pltpu.make_async_remote_copy(
+                        src_ref=ref.at[t], dst_ref=ref.at[t], send_sem=g_send.at[k, j - 1], recv_sem=g_recv.at[k, j - 1],
+                        device_id=(z, ts[j]), device_id_type=MESH)
+                    copy.start()
+                    spread.append(copy)
+    keep_b(n - 1)
+    for copy in sent_b + spread:
+        copy.wait()
+    for copies in sent_a:
+        for copy in copies:
+            copy.wait_send()
+    for copy in small:
+        copy.wait_send()
+    for copy in outs_b:
+        copy.wait()
+
+
+def score(ids_ref, tgt_ref, hid_ref, w_ref, mid_ref, head_ref, out_ref, peak, mass, pick):
+    step = pl.program_id(0)
+
+    @pl.when(step == 0)
+    def _():
+        peak[...] = jnp.full_like(peak, LOWEST)
+        mass[...] = jnp.zeros_like(mass)
+        pick[...] = jnp.zeros_like(pick)
+
+    head_ref[...] = mid_ref[...]
+    logits = lax.dot_general(w_ref[...], hid_ref[...], (((1,), (1,)), ((), ())), preferred_element_type=jnp.float32)
+    ids = ids_ref[...]
+    pick[...] += jnp.sum(jnp.where(ids == tgt_ref[...], logits, 0.0), axis=0, keepdims=True)
+    logits = jnp.where(ids >= 0, logits, LOWEST)
+    old = peak[...]
+    new = jnp.maximum(old, jnp.max(logits, axis=0, keepdims=True))
+    mass[...] = mass[...] * jnp.exp(old - new) + jnp.sum(jnp.exp(logits - new), axis=0, keepdims=True)
+    peak[...] = new
+
+    @pl.when(step == pl.num_programs(0) - 1)
+    def _():
+        out_ref[0:1, :] = peak[...]
+        out_ref[1:2, :] = mass[...]
+        out_ref[2:3, :] = pick[...]
+        out_ref[3:8, :] = jnp.zeros((5, out_ref.shape[1]), jnp.float32)
+
+
+def shards(n_dp, n_tp, head_fsdp, hidden, targets):
+    width, vocab = head_fsdp.shape
+    if width % 128 or (vocab // n_tp) % 8 or hidden.shape[0] % 8:
+        return plain_shards(head_fsdp, hidden, targets)
+    own, model = hidden.shape
+    columns = vocab // n_tp
+    batch = own * n_dp * n_tp
+    steps, part = plan(columns, n_dp, CHUNKS)
+    n = len(steps)
+    lanes = round_up(own, 128)
+    tgt = jnp.broadcast_to(jnp.pad(targets, (0, lanes - own))[None, :], (8, lanes))
+    anyspace = pl.BlockSpec(memory_space=pl.ANY)
+    bf16 = jnp.bfloat16
+    dma = pltpu.SemaphoreType.DMA
+    mid, full, all_hid, all_tgt = pl.pallas_call(
+        functools.partial(exchange, n_dp, n_tp, steps),
+        out_shape=[
+            jax.ShapeDtypeStruct((columns, n_tp * width), bf16),
+            jax.ShapeDtypeStruct((part, model), bf16),
+            jax.ShapeDtypeStruct((n_tp, n_dp, own, model), bf16),
+            jax.ShapeDtypeStruct((n_tp, n_dp, 8, lanes), jnp.int32),
+        ],
+        in_specs=[anyspace] * 3,
+        out_specs=[anyspace] * 4,
+        scratch_shapes=[
+            pltpu.VMEM((columns, width), bf16),
+            pltpu.VMEM((part, n_tp * width), bf16),
+            pltpu.VMEM((own, model), bf16),
+            pltpu.VMEM((8, lanes), jnp.int32),
+            dma((n, n_tp - 1)), dma((n, n_tp - 1)),
+            dma((n, n_dp - 1)), dma((n, n_dp - 1)),
+            dma((2, n_dp - 1)), dma((2, n_dp - 1)),
+            dma((2, n_tp - 1)), dma((2, n_tp - 1)),
+            dma((5, max(n, 4))),
+        ],
+        compiler_params=pltpu.CompilerParams(
+            collective_id=0, has_side_effects=True, vmem_limit_bytes=60 * 2**20),
+        name="exchange",
+    )(head_fsdp.T, hidden, tgt)
+
+    z, t = lax.axis_index("dp"), lax.axis_index("tp")
+    grid = -(-part // TILE)
+    ids = []
+    for start, rows, share, _ in steps:
+        first = jnp.minimum(z * share, rows - share)
+        row = first + jnp.arange(share, dtype=jnp.int32)
+        ids.append(jnp.where(row >= z * share, t * columns + start + row, -1))
+    ids = jnp.pad(jnp.concatenate(ids), (0, grid * TILE - part), constant_values=-1)[:, None]
+    all_targets = all_tgt[:, :, 0, :own].reshape(1, batch)
+    keep = round_up(-(-columns // grid), 16)
+    head_t, local = pl.pallas_call(
+        score,
+        grid=(grid,),
+        out_shape=[
+            jax.ShapeDtypeStruct((columns, n_tp * width), bf16),
+            jax.ShapeDtypeStruct((8, batch), jnp.float32),
+        ],
+        in_specs=[
+            pl.BlockSpec((TILE, 1), lambda i: (i, 0)),
+            pl.BlockSpec((1, batch), lambda i: (0, 0)),
+            pl.BlockSpec((batch, model), lambda i: (0, 0), pipeline_mode=pl.Buffered(1)),
+            pl.BlockSpec((TILE, model), lambda i: (i, 0)),
+            pl.BlockSpec((keep, n_tp * width), lambda i: (i, 0)),
+        ],
+        out_specs=[
+            pl.BlockSpec((keep, n_tp * width), lambda i: (i, 0)),
+            pl.BlockSpec((8, batch), lambda i: (0, 0)),
+        ],
+        scratch_shapes=[pltpu.VMEM((1, batch), jnp.float32)] * 3,
+        compiler_params=pltpu.CompilerParams(vmem_limit_bytes=60 * 2**20),
+        name="score",
+    )(ids, all_targets, all_hid.reshape(batch, model), full, mid)
+
+    pieces = local[:3].reshape(3, n_tp, n_dp, own).transpose(2, 1, 0, 3).reshape(n_dp * n_tp, 3 * own)
+    pieces = lax.all_to_all(pieces, ("dp", "tp"), split_axis=0, concat_axis=0, tiled=True)
+    peaks, masses, picks = (pieces[:, i * own:(i + 1) * own] for i in range(3))
+    top = jnp.max(peaks, axis=0)
+    log_norm = top + jnp.log(jnp.sum(masses * jnp.exp(peaks - top[None, :]), axis=0))
+    return head_t.T, log_norm, jnp.sum(picks, axis=0) - log_norm
+
+
+def plain_shards(head_fsdp, hidden, targets):
     head_tp = lax.all_to_all(head_fsdp, "tp", split_axis=1, concat_axis=0, tiled=True)
     head_full = lax.all_to_all(head_fsdp, ("dp", "tp"), split_axis=1, concat_axis=0, tiled=True)
     vocab_start = (
@@ -34,4 +290,5 @@
 def solution(mesh):
     in_specs = (P(("dp", "tp"), None), P(("dp", "tp"), None), P(("dp", "tp")))
     out_specs = (P("dp", "tp"), P(("dp", "tp")), P(("dp", "tp")))
-    return jax.shard_map(shards, mesh=mesh, in_specs=in_specs, out_specs=out_specs, check_vma=False)
+    body = functools.partial(shards, mesh.shape["dp"], mesh.shape["tp"])
+    return jax.shard_map(body, mesh=mesh, in_specs=in_specs, out_specs=out_specs, check_vma=False)

time: 1470 us -> 861 us (0.59)
  blocking collectives: 1230 us -> 32.3 us
  Pallas kernels: 0 us -> 778 us
  local copies, waits for them, and re-layouts: 166 us -> 47.8 us
  matrix products: 42.3 us -> 0 us
    unnamed x1 -> x0, blocking collectives: 779 us -> none
    pallas_call x0 -> x2, Pallas kernels: none -> 778 us  [the longest x1 728 us: shards(): pl.pallas_call(functools.partial(exchange, n_dp, n_tp, steps), out_shape=...]
    all_to_all x1, blocking collectives: 368 us -> 32.3 us  [shards(): lax.all_to_all(pieces, ('dp', 'tp'), split_axis=0, concat_axis=0, tiled=T...]
    all_to_all x2 -> x1, local copies, waits for them, and re-layouts: 79.6 us -> 0.09 us  [shards(): lax.all_to_all(pieces, ('dp', 'tp'), split_axis=0, concat_axis=0, tiled=T...]
    unnamed x6 -> x3, local copies, waits for them, and re-layouts: 85.3 us -> 42.5 us
    dot_general x1 -> x0, matrix products: 42.3 us -> none  [shards(): logits = jnp.dot(all_hidden, head_full, preferred_element_type=jnp.float32)]
    psum x1 -> x0, blocking collectives: 42.1 us -> none  [shards(): total_mass, target_logit = lax.psum((local_mass, picked), ('dp', 'tp'))]
    pmax x1 -> x0, blocking collectives: 37.9 us -> none  [shards(): top_logit = lax.pmax(local_peak, ('dp', 'tp'))]
  transfers between devices with their start and end apart: 2 -> 0, of which waited for: 0 -> 0; matrix products, arithmetic and copies ran while one was open for 8% -> 0% of each run, Pallas kernels for 0% -> 0%
where the time goes in v1:
time: 861 us; the launch traced here: 859 us
  Pallas kernels  778 us (90%)
  local copies, waits for them, and re-layouts  47.8 us (6%)
  blocking collectives  32.3 us (4%)
    pallas_call x1, Pallas kernels, shards(): pl.pallas_call(functools.partial(exchange, n_dp, n_tp, steps), out_shape=...  728 us
    pallas_call x1, Pallas kernels, shards(): pl.pallas_call(score, grid=(grid,), out_shape=[jax.ShapeDtypeStruct((colu...  49.7 us
    unnamed x3, local copies, waits for them, and re-layouts  42.5 us
    all_to_all x1, blocking collectives, shards(): lax.all_to_all(pieces, ('dp', 'tp'), split_axis=0, concat_axis=0, tiled=T...  32.3 us

profile of v1, /device:TPU:0, one launch (start us, length us, event | category | flops | bytes accessed | tf_op | source)
XLA Modules:
  0.0 859.2 jit_solution(8921957967456631809)
XLA Ops:
  0.7 0.1 concatenate.3
  0.8 2.0 copy.11.ids_ref
  2.8 0.0 copy-start
  2.8 42.5 %copy.10 = bf16[128,128256]{0,1:T(8,128)(2,1)} copy(bf16[128,128256]{1,0:T(8,128)(2,1)} %param.3) | data formatting | bytes 65667072 | tf_op args[0]
  45.3 0.0 copy-done
  45.3 0.6 broadcast_in_dim.27.tgt
  45.9 728.0 %exchange.1 = (bf16[16032,1024]{1,0:T(8,128)(2,1)}, bf16[4008,4096]{1,0:T(8,128)(2,1)}, bf16[8,4,32,4096]{3,2,1,0:T(8,128)(2,1)}, s32[8,4,8,128]{3,2,1,0:T(8,128)}) custom-call(bf16[128256,128]{1,0:T(8,128)(2,1)} %bitcast.9, bf16[32,4096]{1,0:T(8,128)(2,1)} %hid.1, s32[8,128]{1,0:T(8,128)} %broadcast_in_dim.27.tgt), custom_call_target="tpu_custom_call" | custom-call | tf_op jit(solution)/shard_map/exchange/pallas_call | solution.py:196
  773.9 1.0 slice_reduce_fusion.1
  774.9 0.7 reshape_squeeze.3.tgt_ref
  775.6 49.7 %score.1 = (bf16[16032,1024]{1,0:T(8,128)(2,1)}, f32[8,1024]{1,0:T(8,128)}) custom-call(s32[4096,1]{1,0:T(8,128)} %copy.11.ids_ref, s32[1,1024]{1,0:T(1,128)} %reshape_squeeze.3.tgt_ref, bf16[1024,4096]{1,0:T(8,128)(2,1)} %bitcast.10, bf16[4008,4096]{1,0:T(8,128)(2,1)} %get-tuple-element.11.w_ref, bf16[16032,1024]{1,0:T(8,128)(2,1)} %get-tuple-element.12.mid_ref), custom_call_target="tpu_custom_call" | custom-call | tf_op jit(solution)/shard_map/score/pallas_call | solution.py:232
  825.3 0.8 slice.16
  826.1 0.1 reshape.19
  826.2 0.1 all_to_all.8
  826.3 32.3 %all_to_all.12 = f32[32,1,96]{2,1,0:T(1,128)S(1)} all-to-all(f32[32,1,96]{2,1,0:T(1,128)S(1)} %bitcast.15), channel_id=1, replica_groups=mesh['dp'=4,'tp'=8] {'dp','tp'}, dimensions={0} | all-to-all | bytes 24576 | tf_op jit(solution)/shard_map/all_to_all | solution.py:256
  858.6 0.1 slice_reduce_fusion
  858.7 0.5 fusion.3
  (9 shorter events, 0.1 us)
Async XLA Ops:
  2.8 42.5 %copy-start = (s32[32]{0:T(128)S(1)}, s32[32]{0:T(128)}, u32[]{:S(2)}) copy-start(s32[32]{0:T(128)} %param.5) | copy-start | bytes 388

commit v2 on v1

--- a/solution.py
+++ b/solution.py
@@ -19,7 +19,8 @@
 
 
 def plan(columns, n_dp, chunks):
-    share = round_up(-(-columns // (n_dp * chunks)), 8)
+    full_share = round_up(-(-columns // (n_dp * chunks)), 8)
+    share = round_up(-(-full_share // 8), 8)
     steps, start, place = [], 0, 0
     while start < columns:
         rows = min(share * n_dp, columns - start)
@@ -27,6 +28,7 @@
         steps.append((start, rows, part, place))
         start += rows
         place += part
+        share = min(2 * share, full_share)
     return steps, place
 
 
@@ -34,11 +36,20 @@
     return pl.multiple_of(jnp.minimum(peer * part, rows - part), 8)
 
 
-def exchange(n_dp, n_tp, steps, head, hid, tgt, mid, full, all_hid, all_tgt, own_a, own_b, own_h, own_t,
+def spans(steps):
+    out, place = [], 0
+    for _, rows, _, _ in steps:
+        length = round_up(rows + 120, 128)
+        out.append((place, length))
+        place += length
+    return out, place
+
+
+def exchange(n_dp, n_tp, steps, head, hid, tgt, mid, full, all_hid, all_tgt, stage, cols_in, rows_out, t_sem, own_a, own_b, own_h, own_t,
              a_send, a_recv, b_send, b_recv, h_send, h_recv, g_send, g_recv, local):
     z, t = lax.axis_index("dp"), lax.axis_index("tp")
     depth = hid.shape[0]
-    width = head.shape[1]
+    width, vocab = head.shape
     columns = mid.shape[0]
     zs = [lax.rem(z + j, n_dp) for j in range(n_dp)]
     ts = [lax.rem(t + j, n_tp) for j in range(n_tp)]
@@ -51,29 +62,64 @@
     lane = pl.ds(pl.multiple_of(t * width, width), width)
     block = pl.ds(pl.multiple_of(z * mid.shape[1], mid.shape[1]), mid.shape[1])
 
-    loads = []
-    for c, (start, rows, part, place) in enumerate(steps):
-        copy = pltpu.make_async_copy(
-            head.at[pl.ds(pl.multiple_of(t * columns + start, 8), rows)], own_a.at[pl.ds(start, rows)], local.at[0, c])
-        copy.start()
-        loads.append(copy)
+    places, _ = spans(steps)
+
+    def source(c, j):
+        start, rows, _, _ = steps[c]
+        place, length = places[c]
+        first = ts[j] * columns + start
+        base = jnp.minimum(first // 128 * 128, vocab - length)
+        return base, stage.at[j, pl.ds(pl.multiple_of(place + first - base, 8), rows)]
+
+    def turn(c):
+        place, length = places[c]
+        copies = []
+        for j in range(n_tp):
+            base, _ = source(c, j)
+            copy = pltpu.make_async_copy(
+                head.at[:, pl.ds(pl.multiple_of(base, 128), length)], cols_in.at[j, :, pl.ds(0, length)], t_sem.at[0, j])
+            copy.start()
+            copies.append(copy)
+        outs = []
+        for j in range(n_tp):
+            copies[j].wait()
+
+            def tile(k, carry, j=j):
+                at = pl.ds(pl.multiple_of(k * 128, 128), 128)
+                rows_out[j, at, :] = cols_in[j, :, at].T
+                return carry
+
+            lax.fori_loop(0, length // 128, tile, 0)
+            copy = pltpu.make_async_copy(
+                rows_out.at[j, pl.ds(0, length)], stage.at[j, pl.ds(place, length)], t_sem.at[1, j])
+            copy.start()
+            outs.append(copy)
+        for copy in outs:
+            copy.wait()
+
     in_h = pltpu.make_async_copy(hid, own_h, local.at[4, 0])
     in_t = pltpu.make_async_copy(tgt, own_t, local.at[4, 1])
     in_h.start()
     in_t.start()
     pl.semaphore_wait(barrier, n_dp + n_tp - 2)
 
+    loads = []
+
     def send_a(c):
         start, rows, part, place = steps[c]
+        turn(c)
         copies = []
         for j in range(1, n_tp):
             copy = pltpu.make_async_remote_copy(
-                src_ref=head.at[pl.ds(pl.multiple_of(ts[j] * columns + start, 8), rows)],
+                src_ref=source(c, j)[1],
                 dst_ref=mid.at[pl.ds(start, rows), lane],
                 send_sem=a_send.at[c, j - 1], recv_sem=a_recv.at[c, j - 1],
                 device_id=(z, ts[j]), device_id_type=MESH)
             copy.start()
             copies.append(copy)
+        copy = pltpu.make_async_copy(source(c, 0)[1], own_a.at[pl.ds(start, rows)], local.at[0, c])
+        copy.start()
+        loads.append(copy)
         return copies
 
     sent_a = [send_a(c) for c in range(min(AHEAD, n))]
@@ -92,13 +138,6 @@
     out_t = pltpu.make_async_copy(own_t, all_tgt.at[t, z], local.at[4, 3])
     out_h.start()
     out_t.start()
-    stores = []
-    for c, (start, rows, part, place) in enumerate(steps):
-        loads[c].wait()
-        copy = pltpu.make_async_copy(own_a.at[pl.ds(start, rows)], mid.at[pl.ds(start, rows), lane], local.at[1, c])
-        copy.start()
-        stores.append(copy)
-
     sent_b, ins_b, outs_b, spread = [], [], [], []
 
     def keep_b(c):
@@ -109,7 +148,10 @@
         outs_b.append(copy)
 
     for c, (start, rows, part, place) in enumerate(steps):
-        stores[c].wait()
+        loads[c].wait()
+        store = pltpu.make_async_copy(own_a.at[pl.ds(start, rows)], mid.at[pl.ds(start, rows), lane], local.at[1, c])
+        store.start()
+        store.wait()
         for copy in sent_a[c]:
             copy.wait_recv()
         for j in range(1, n_dp):
@@ -181,7 +223,7 @@
 
 def shards(n_dp, n_tp, head_fsdp, hidden, targets):
     width, vocab = head_fsdp.shape
-    if width % 128 or (vocab // n_tp) % 8 or hidden.shape[0] % 8:
+    if width != 128 or vocab % 128 or (vocab // n_tp) % 8 or hidden.shape[0] % 8:
         return plain_shards(head_fsdp, hidden, targets)
     own, model = hidden.shape
     columns = vocab // n_tp
@@ -193,17 +235,23 @@
     anyspace = pl.BlockSpec(memory_space=pl.ANY)
     bf16 = jnp.bfloat16
     dma = pltpu.SemaphoreType.DMA
-    mid, full, all_hid, all_tgt = pl.pallas_call(
+    _, staged = spans(steps)
+    widest = max(length for _, length in spans(steps)[0])
+    mid, full, all_hid, all_tgt, _ = pl.pallas_call(
         functools.partial(exchange, n_dp, n_tp, steps),
         out_shape=[
             jax.ShapeDtypeStruct((columns, n_tp * width), bf16),
             jax.ShapeDtypeStruct((part, model), bf16),
             jax.ShapeDtypeStruct((n_tp, n_dp, own, model), bf16),
             jax.ShapeDtypeStruct((n_tp, n_dp, 8, lanes), jnp.int32),
+            jax.ShapeDtypeStruct((n_tp, staged, width), bf16),
         ],
         in_specs=[anyspace] * 3,
-        out_specs=[anyspace] * 4,
+        out_specs=[anyspace] * 5,
         scratch_shapes=[
+            pltpu.VMEM((n_tp, width, widest), bf16),
+            pltpu.VMEM((n_tp, widest, width), bf16),
+            dma((2, n_tp)),
             pltpu.VMEM((columns, width), bf16),
             pltpu.VMEM((part, n_tp * width), bf16),
             pltpu.VMEM((own, model), bf16),
@@ -217,7 +265,7 @@
         compiler_params=pltpu.CompilerParams(
             collective_id=0, has_side_effects=True, vmem_limit_bytes=60 * 2**20),
         name="exchange",
-    )(head_fsdp.T, hidden, tgt)
+    )(head_fsdp, hidden, tgt)
 
     z, t = lax.axis_index("dp"), lax.axis_index("tp")
     grid = -(-part // TILE)

time: 861 us -> 820 us (0.952)
  local copies, waits for them, and re-layouts: 47.8 us -> 5.95 us
  Pallas kernels: 778 us -> 801 us
  blocking collectives: 32.3 us -> 11 us
    unnamed x3 -> x0, local copies, waits for them, and re-layouts: 42.5 us -> none
    pallas_call x1, Pallas kernels: 728 us -> 751 us  [shards(): pl.pallas_call(functools.partial(exchange, n_dp, n_tp, steps), out_shape=...]
    all_to_all x1, blocking collectives: 32.3 us -> 11 us  [shards(): lax.all_to_all(pieces, ('dp', 'tp'), split_axis=0, concat_axis=0, tiled=T...]
where the time goes in v2:
time: 820 us; the launch traced here: 819 us
  Pallas kernels  801 us (98%)
  blocking collectives  11 us (1%)
    pallas_call x1, Pallas kernels, shards(): pl.pallas_call(functools.partial(exchange, n_dp, n_tp, steps), out_shape=...  751 us
    pallas_call x1, Pallas kernels, shards(): pl.pallas_call(score, grid=(grid,), out_shape=[jax.ShapeDtypeStruct((colu...  49.7 us

profile of v2, /device:TPU:0, one launch (start us, length us, event | category | flops | bytes accessed | tf_op | source)
XLA Modules:
  0.0 819.5 jit_solution(8414083207119120724)
XLA Ops:
  0.8 0.1 concatenate.3
  0.9 2.0 copy.8.ids_ref
  2.9 0.7 pad.9
  3.5 0.6 broadcast_in_dim.42.tgt
  4.1 751.3 %exchange.1 = (bf16[16032,1024]{1,0:T(8,128)(2,1)}, bf16[4008,4096]{1,0:T(8,128)(2,1)}, bf16[8,4,32,4096]{3,2,1,0:T(8,128)(2,1)}, s32[8,4,8,128]{3,2,1,0:T(8,128)}, bf16[8,17664,128]{2,1,0:T(8,128)(2,1)}) custom-call(bf16[128,128256]{1,0:T(8,128)(2,1)} %head.1, bf16[32,4096]{1,0:T(8,128)(2,1)} %hid.1, s32[8,128]{1,0:T(8,128)} %broadcast_in_dim.42.tgt), custom_call_target="tpu_custom_call" | custom-call | tf_op jit(solution)/shard_map/exchange/pallas_call | solution.py:240
  755.4 1.0 slice_reduce_fusion.1
  756.4 0.7 reshape_squeeze.3.tgt_ref
  757.0 49.7 %score.1 = (bf16[16032,1024]{1,0:T(8,128)(2,1)}, f32[8,1024]{1,0:T(8,128)}) custom-call(s32[4096,1]{1,0:T(8,128)} %copy.8.ids_ref, s32[1,1024]{1,0:T(1,128)} %reshape_squeeze.3.tgt_ref, bf16[1024,4096]{1,0:T(8,128)(2,1)} %bitcast.8, bf16[4008,4096]{1,0:T(8,128)(2,1)} %get-tuple-element.11.w_ref, bf16[16032,1024]{1,0:T(8,128)(2,1)} %get-tuple-element.12.mid_ref), custom_call_target="tpu_custom_call" | custom-call | tf_op jit(solution)/shard_map/score/pallas_call | solution.py:280
  806.8 0.8 slice.16
  807.5 0.1 reshape.19
  807.7 0.1 all_to_all.8
  807.8 11.0 %all_to_all.12 = f32[32,1,96]{2,1,0:T(1,128)S(1)} all-to-all(f32[32,1,96]{2,1,0:T(1,128)S(1)} %bitcast.13), channel_id=1, replica_groups=mesh['dp'=4,'tp'=8] {'dp','tp'}, dimensions={0} | all-to-all | bytes 24576 | tf_op jit(solution)/shard_map/all_to_all | solution.py:304
  818.8 0.1 slice_reduce_fusion
  818.9 0.5 fusion.2
  (11 shorter events, 0.1 us)
